TPU v7x, 128 devices: a whole 4x4x4 slice. The times are simulated.
128 devices in a mesh: rep: 4 (over z_lo, core), shard: 32 (over z_hi, y, x).
Axes of the slice: x: 4, y: 4, z: 4 (z_hi: 2, z_lo: 2; z = z_hi * 2 + z_lo), core: 2. Of those that a mesh axis runs over, the one named last changes fastest.
Arguments:
- inputs: float32 [32, 512, 1024], P('shard', 'rep'), may hold values from -6 to 6
- segment_ids: int32 [32, 512], P('shard', 'rep'), may hold values from 0 to 3, never falling along the last dimension, each value on 1 to 200 neighbouring positions
- cotangent: float32 [32, 512, 1024], P('shard', 'rep'), may hold values from -6 to 6
- w_qkv: bfloat16 [1, 1024, 3072], P(None, 'shard'), may hold values from -0.1875 to 0.1875
- w_out: bfloat16 [1, 1024, 1024], P(None, 'shard'), may hold values from -0.75 to 0.75
- w_up: bfloat16 [1, 1024, 4096], P(None, 'shard'), may hold values from -0.1875 to 0.1875
- w_down: bfloat16 [1, 4096, 1024], P(None, 'shard'), may hold values from -0.09375 to 0.09375
- biases: bfloat16 [1, 6, 1024], P(None, None, 'shard'), may hold values from -3 to 3
- norm_gains: bfloat16 [1, 2, 1024], P(None, None, 'shard'), may hold values from 0.5 to 1.5
- up_bias: bfloat16 [1, 4096], P(None, 'shard'), may hold values from -3 to 3
Outputs:
- outputs: float32 [32, 512, 1024], P('shard', 'rep')
- input_grad: float32 [32, 512, 1024], P('shard', 'rep')
- grad_w_qkv: float32 [1, 1024, 3072], P(None, 'shard')
- grad_w_out: float32 [1, 1024, 1024], P(None, 'shard')
- grad_w_up: float32 [1, 1024, 4096], P(None, 'shard')
- grad_w_down: float32 [1, 4096, 1024], P(None, 'shard')
- grad_biases: float32 [1, 6, 1024], P(None, None, 'shard')
- grad_norm_gains: float32 [1, 2, 1024], P(None, None, 'shard')
- grad_up_bias: float32 [1, 4096], P(None, 'shard')
Inputs may be any that keep to these rules, and one draw needn't show every extreme that they name: `segment_ids`: within each sequence the id never falls along the positions; ids of different sequences are unrelated.
All inputs are finite; a program needn't handle non-finite values.
Results may differ from a plain program's by a relative error of at most 0.025.
Values may be sent and summed in bfloat16 or wider, within the bound.
A program may use at most 128 MiB of HBM per device.

v0:
```python
import math
import jax
import jax.numpy as jnp
from jax import lax
from jax.sharding import PartitionSpec as P

D = 1024
HEADS = 16
HEAD_DIM = 64
LAYERS = 1
epsilon = 1e-06


def normalize(residual):
    center = residual - jnp.mean(residual, axis=-1, keepdims=True)
    rstd_val = lax.rsqrt(jnp.mean(center * center, axis=-1, keepdims=True) + epsilon)
    return (center * rstd_val, rstd_val)


def norm_back(grad_out, x_hat, rstd_val, gain_row):
    d_hat = grad_out * gain_row
    return rstd_val * (
        d_hat
        - jnp.mean(d_hat, axis=-1, keepdims=True)
        - x_hat * jnp.mean(d_hat * x_hat, axis=-1, keepdims=True)
    )


def gelu_pair(pre_act):
    normal_cdf = 0.5 * (1.0 + lax.erf(pre_act * (1.0 / math.sqrt(2.0))))
    density = jnp.exp(-0.5 * pre_act * pre_act) * (1.0 / math.sqrt(2.0 * math.pi))
    return (pre_act * normal_cdf, normal_cdf + pre_act * density)


def matmul(first_op, second_op):
    return jnp.dot(first_op, second_op, preferred_element_type=jnp.float32)


def matmul_lt(first_op, second_op):
    return lax.dot_general(
        first_op, second_op, (((0,), (0,)), ((), ())), preferred_element_type=jnp.float32
    )


def matmul_rt(first_op, second_op):
    return lax.dot_general(
        first_op, second_op, (((1,), (1,)), ((), ())), preferred_element_type=jnp.float32
    )


def attention_scores(queries, keys_all, seg_rows, seg_cols):
    scores = jnp.einsum(
        "sqhe,skhe->shqk", queries, keys_all, preferred_element_type=jnp.float32
    ) * (1.0 / math.sqrt(HEAD_DIM))
    allowed = seg_rows[:, None, :, None] == seg_cols[:, None, None, :]
    return (scores, allowed)


def pick(tensor, index, axis):
    return lax.dynamic_index_in_dim(tensor, index, axis=axis, keepdims=False)


def pack_cols(tensor, parts):
    rows = tensor.shape[0]
    return tensor.reshape(rows, parts, -1).transpose(1, 0, 2).reshape(parts, -1)


def unpack_cols(flat, parts, rows):
    return flat.reshape(parts, rows, -1).transpose(1, 0, 2).reshape(rows, -1)


def gather_rep(tensor):
    return lax.all_gather(tensor, "rep", axis=0, tiled=True)


def scatter_rep(tensor):
    return lax.psum_scatter(tensor, "rep", scatter_dimension=0, tiled=True)


def local(inputs, segment_ids, cotangent, w_qkv, w_out, w_up, w_down, biases, norm_gains, up_bias):
    parts = lax.axis_size("shard")
    reps = lax.axis_size("rep")
    r = lax.axis_index("rep")
    head_cols = D // reps
    heads_here = HEADS // reps
    ff_all = w_up.shape[2]
    ff_chunk = ff_all // parts
    ff_piece = ff_chunk // reps
    k_rows = D // parts
    qkv_piece = pick(w_qkv[0].reshape(k_rows, 3, reps, head_cols), r, 2).reshape(k_rows, -1)
    out_piece = w_out[0]
    up_piece = pick(w_up[0].reshape(k_rows, parts, reps, ff_piece), r, 2).reshape(k_rows, -1)
    down_piece = pick(w_down[0].reshape(reps, ff_piece, D), r, 0)
    upb_piece = pick(up_bias[0].reshape(reps, ff_piece), r, 0)
    pieces = (qkv_piece, out_piece, up_piece, down_piece, upb_piece, biases[0], norm_gains[0])
    sizes = [piece.size for piece in pieces]
    offsets = [sum(sizes[:i]) for i in range(len(sizes) + 1)]
    packed = jnp.concatenate([piece.reshape(-1) for piece in pieces])
    packed = jnp.pad(packed, (0, -(-packed.size // 1024) * 1024 - packed.size))
    gathered = lax.all_gather(packed, "shard", axis=0, tiled=False)
    got = [gathered[:, offsets[i] : offsets[i + 1]] for i in range(len(sizes))]
    w_qkv_r = got[0].reshape(D, 3 * head_cols)
    w_out_all = got[1].reshape(D, D)
    w_out_r = lax.dynamic_slice_in_dim(w_out_all, r * head_cols, head_cols, axis=0)
    w_up_r = got[2].reshape(D, -1)
    w_down_r = got[3].reshape(-1, D)
    up_bias_r = got[4].reshape(-1)
    bias_all = unpack_cols(got[5], parts, biases.shape[1])
    gain_all = unpack_cols(got[6], parts, norm_gains.shape[1])
    bias_q = lax.dynamic_slice_in_dim(bias_all[0], r * head_cols, head_cols)
    bias_v = lax.dynamic_slice_in_dim(bias_all[1], r * head_cols, head_cols)
    rows_f32 = inputs[0]
    own = rows_f32.shape[0]
    rows_bf = rows_f32.astype(jnp.bfloat16)
    seg_tag = jnp.broadcast_to(segment_ids[0].astype(jnp.bfloat16)[:, None], (own, 128))
    hb_seg = gather_rep(jnp.concatenate([rows_bf, seg_tag], axis=1))
    hb_all = hb_seg[:, :D]
    seg_all = hb_seg[:, D]
    qkv_rows = matmul(hb_all, w_qkv_r)
    queries = (
        (qkv_rows[:, :head_cols] + bias_q).astype(jnp.bfloat16).reshape(1, -1, heads_here, HEAD_DIM)
    )
    keys_all = (
        qkv_rows[:, head_cols : 2 * head_cols]
        .astype(jnp.bfloat16)
        .reshape(1, -1, heads_here, HEAD_DIM)
    )
    values_all = (
        (qkv_rows[:, 2 * head_cols :] + bias_v)
        .astype(jnp.bfloat16)
        .reshape(1, -1, heads_here, HEAD_DIM)
    )
    seg_rows = seg_all[None]
    scores, allowed = attention_scores(queries, keys_all, seg_rows, seg_rows)
    expo_all = jnp.where(allowed, jnp.exp(scores), 0.0)
    row_total = jnp.sum(expo_all, axis=-1, keepdims=True)
    log_total = jnp.log(row_total)
    attn_probs = (expo_all / row_total).astype(jnp.bfloat16)
    context = (
        jnp.einsum("shqk,skhe->sqhe", attn_probs, values_all, preferred_element_type=jnp.float32)
        .astype(jnp.bfloat16)
        .reshape(-1, head_cols)
    )
    first_sum = rows_f32 + scatter_rep(matmul(context, w_out_r)) + bias_all[2]
    norm_one, rstd_one = normalize(first_sum)
    mid_norm = norm_one * gain_all[0] + bias_all[3]
    mid_b = mid_norm.astype(jnp.bfloat16)
    mid_all = gather_rep(mid_b)
    pre_act = matmul(mid_all, w_up_r) + up_bias_r
    act_f32, gelu_slope = gelu_pair(pre_act)
    act_b = act_f32.astype(jnp.bfloat16)
    second_sum = mid_norm + scatter_rep(matmul(act_b, w_down_r)) + bias_all[4]
    norm_two, rstd_two = normalize(second_sum)
    layer_out = norm_two * gain_all[1] + bias_all[5]
    grad_rows = cotangent[0]
    d_gain_two = jnp.sum(grad_rows * norm_two, axis=0)
    d_bias_two = jnp.sum(grad_rows, axis=0)
    d_second = norm_back(grad_rows, norm_two, rstd_two, gain_all[1])
    d_bdown = jnp.sum(d_second, axis=0)
    d_second_all = gather_rep(d_second.astype(jnp.bfloat16))
    d_wdown = matmul_lt(act_b, d_second_all)
    d_pre = matmul_rt(d_second_all, w_down_r) * gelu_slope
    d_bup = jnp.sum(d_pre, axis=0)
    d_pre_b = d_pre.astype(jnp.bfloat16)
    d_wup = matmul_lt(mid_all, d_pre_b)
    ffn_pack = jnp.concatenate(
        [
            d_wup.astype(jnp.bfloat16).reshape(parts, -1),
            d_wdown.astype(jnp.bfloat16).reshape(parts, -1),
        ],
        axis=1,
    ).reshape(parts, 8, -1)
    ffn_recv = lax.all_to_all(ffn_pack, "shard", 0, 0, tiled=True)
    ffn_share = jnp.sum(ffn_recv.astype(jnp.float32), axis=0).astype(jnp.bfloat16)
    d_mid = d_second + scatter_rep(matmul_rt(d_pre_b, w_up_r))
    d_gain_one = jnp.sum(d_mid * norm_one, axis=0)
    d_bias_one = jnp.sum(d_mid, axis=0)
    d_first = norm_back(d_mid, norm_one, rstd_one, gain_all[0])
    d_bout = jnp.sum(d_first, axis=0)
    d_first_all = gather_rep(d_first.astype(jnp.bfloat16))
    d_wout = matmul_lt(context, d_first_all)
    d_context = (
        matmul_rt(d_first_all, w_out_r).astype(jnp.bfloat16).reshape(1, -1, heads_here, HEAD_DIM)
    )
    probs_again = jnp.where(allowed, jnp.exp(scores - log_total), 0.0)
    d_probs = jnp.einsum(
        "sqhe,skhe->shqk", d_context, values_all, preferred_element_type=jnp.float32
    )
    d_scores = (
        probs_again
        * (d_probs - jnp.sum(probs_again * d_probs, axis=-1, keepdims=True))
        * (1.0 / math.sqrt(HEAD_DIM))
    ).astype(jnp.bfloat16)
    d_queries = jnp.einsum(
        "shqk,skhe->sqhe", d_scores, keys_all, preferred_element_type=jnp.float32
    ).reshape(-1, head_cols)
    d_keys = jnp.einsum(
        "shqk,sqhe->skhe", d_scores, queries, preferred_element_type=jnp.float32
    ).reshape(-1, head_cols)
    d_values = jnp.einsum(
        "shqk,sqhe->skhe",
        probs_again.astype(jnp.bfloat16),
        d_context,
        preferred_element_type=jnp.float32,
    ).reshape(-1, head_cols)
    d_qkv = jnp.concatenate([d_queries, d_keys, d_values], axis=-1).astype(jnp.bfloat16)
    d_wqkv = matmul_lt(hb_all, d_qkv)
    input_grad = d_first + scatter_rep(matmul_rt(d_qkv, w_qkv_r))
    zeros_cols = jnp.zeros((D,), jnp.float32)
    d_bq = lax.dynamic_update_slice_in_dim(zeros_cols, jnp.sum(d_queries, axis=0), r * head_cols, 0)
    d_bv = lax.dynamic_update_slice_in_dim(zeros_cols, jnp.sum(d_values, axis=0), r * head_cols, 0)
    d_biases = jnp.stack([d_bq, d_bv, d_bout, d_bias_one, d_bdown, d_bias_two])
    d_gains = jnp.stack([d_gain_one, d_gain_two])
    d_wout_all = lax.dynamic_update_slice_in_dim(
        jnp.zeros((D, D), jnp.bfloat16), d_wout.astype(jnp.bfloat16), r * head_cols, 0
    )
    d_bup_all = lax.dynamic_update_slice_in_dim(
        jnp.zeros((parts, reps, ff_piece), jnp.float32), d_bup.reshape(parts, 1, ff_piece), r, 1
    )
    grad_parts = (
        d_wqkv.astype(jnp.bfloat16).reshape(parts, -1),
        d_wout_all.reshape(parts, -1),
        d_bup_all.astype(jnp.bfloat16).reshape(parts, -1),
        pack_cols(d_biases.astype(jnp.bfloat16), parts),
        pack_cols(d_gains.astype(jnp.bfloat16), parts),
    )
    g_sizes = [piece.shape[1] for piece in grad_parts]
    grad_pack = jnp.concatenate(grad_parts, axis=1)
    width = grad_pack.shape[1]
    padded = -(-width // 1024) * 1024
    grad_pack = jnp.pad(grad_pack, ((0, 0), (0, padded - width))).reshape(parts, 8, -1)
    received = lax.all_to_all(grad_pack, "shard", 0, 0, tiled=True)
    shares = jnp.sum(received.astype(jnp.float32), axis=0).astype(jnp.bfloat16)
    all_shares = jnp.concatenate([shares.reshape(-1), ffn_share.reshape(-1)])
    joined = lax.all_gather(all_shares, "rep", axis=0, tiled=False).astype(jnp.float32)
    g_sizes = g_sizes + [padded - width, ffn_share.size // 2, ffn_share.size // 2]
    names = ["qkv", "out", "bup", "bias", "gain", "pad", "up", "down"]
    g_offsets = [sum(g_sizes[:i]) for i in range(len(g_sizes) + 1)]
    got = {names[i]: joined[:, g_offsets[i] : g_offsets[i + 1]] for i in range(len(g_sizes))}
    grad_w_qkv = (
        got["qkv"].reshape(reps, k_rows, 3, head_cols).transpose(1, 2, 0, 3).reshape(k_rows, -1)
    )
    grad_w_out = jnp.sum(got["out"], axis=0).reshape(k_rows, D)
    grad_w_up = (
        got["up"].reshape(reps, k_rows, parts, ff_piece).transpose(1, 2, 0, 3).reshape(k_rows, -1)
    )
    grad_w_down = got["down"].reshape(reps * ff_piece, D)
    grad_up_bias = jnp.sum(got["bup"], axis=0)
    grad_biases = jnp.sum(got["bias"], axis=0).reshape(biases.shape[1], -1)
    grad_gains = jnp.sum(got["gain"], axis=0).reshape(norm_gains.shape[1], -1)
    return (
        layer_out[None],
        input_grad[None],
        grad_w_qkv[None],
        grad_w_out[None],
        grad_w_up[None],
        grad_w_down[None],
        grad_biases[None],
        grad_gains[None],
        grad_up_bias[None],
    )


def solution(mesh):
    in_specs = (
        P("shard", "rep", None),
        P("shard", "rep"),
        P("shard", "rep", None),
        P(None, "shard", None),
        P(None, "shard", None),
        P(None, "shard", None),
        P(None, "shard", None),
        P(None, None, "shard"),
        P(None, None, "shard"),
        P(None, "shard"),
    )
    out_specs = (
        P("shard", "rep", None),
        P("shard", "rep", None),
        P(None, "shard", None),
        P(None, "shard", None),
        P(None, "shard", None),
        P(None, "shard", None),
        P(None, None, "shard"),
        P(None, None, "shard"),
        P(None, "shard"),
    )
    return jax.shard_map(local, mesh=mesh, in_specs=in_specs, out_specs=out_specs, check_vma=False)
```

profile of v0, /device:TPU:1, one launch (start us, length us, event | category | flops | bytes accessed | tf_op | source)
XLA Modules:
  0.0 512.8 jit_solution(16374503692966600030)
XLA Ops:
  17.1 18.4 %all-gather.8.cloned.1.call-done = bf16[512,1152]{1,0:T(8,128)(2,1)} async-done(((bf16[128,1152]{1,0:T(8,128)(2,1)}), bf16[512,1152]{1,0:T(8,128)(2,1)}) %all-gather.8.cloned.1.call-update) | async-done | bytes 1179664 | tf_op jit(solution)/shard_map/all_gather | solution.py:73
  37.5 104.4 %all-gather.16.cloned.1.call-done = bf16[3964928]{0:T(1024)(128)(2,1)} async-done(((bf16[123904]{0:T(1024)(128)(2,1)}), bf16[3964928]{0:T(1024)(128)(2,1)}) %all-gather.16.cloned.1.call-update) | async-done | bytes 7929872 | tf_op jit(solution)/shard_map/all_gather | solution.py:100
  141.9 8.3 %reshape.394 = bf16[32,123904]{1,0:T(8,128)(2,1)} reshape(bf16[3964928]{0:T(1024)(128)(2,1)} %all-gather.16.cloned.1.call-done) | data formatting | bytes 15859712 | tf_op jit(solution)/shard_map/all_gather | solution.py:100
  151.1 5.7 %fusion.76 = (bf16[32,32768]{1,0:T(8,128)(2,1)}, bf16[32,32768]{1,0:T(8,128)(2,1)}, bf16[32,32768]{1,0:T(8,128)(2,1)}) fusion(bf16[32,123904]{1,0:T(8,128)(2,1)} %reshape.394), kind=kLoop, calls=%fused_computation.142 | loop fusion | bytes 12582912 | tf_op jit(solution)/shard_map/slice | solution.py:101
  172.9 25.4 %reduce-scatter.5.cloned.1.call-done = f32[128,1024]{1,0:T(8,128)} async-done(((f32[512,1024]{1,0:T(8,128)}), f32[128,1024]{1,0:T(8,128)}) %reduce-scatter.5.cloned.1.call-update) | async-done | bytes 524304 | tf_op jit(solution)/shard_map/reduce_scatter | solution.py:77
  201.9 4.3 reshape.370
  208.6 14.1 %all-gather.10.cloned.1.call-done = bf16[512,1024]{1,0:T(8,128)(2,1)} async-done(((bf16[128,1024]{1,0:T(8,128)(2,1)}), bf16[512,1024]{1,0:T(8,128)(2,1)}) %all-gather.10.cloned.1.call-update) | async-done | bytes 1048592 | tf_op jit(solution)/shard_map/all_gather | solution.py:73
  222.7 4.6 multiply_convert_fusion.1
  231.1 29.0 %reduce-scatter.7.cloned.1.call-done = f32[128,1024]{1,0:T(8,128)} async-done(((f32[512,1024]{1,0:T(8,128)}), f32[128,1024]{1,0:T(8,128)}) %reduce-scatter.7.cloned.1.call-update) | async-done | bytes 524304 | tf_op jit(solution)/shard_map/reduce_scatter | solution.py:77
  263.8 22.0 %all-gather.12.cloned.1.call-done = bf16[512,1024]{1,0:T(8,128)(2,1)} async-done(((bf16[128,1024]{1,0:T(8,128)(2,1)}), bf16[512,1024]{1,0:T(8,128)(2,1)}) %all-gather.12.cloned.1.call-update) | async-done | bytes 1048592 | tf_op jit(solution)/shard_map/all_gather | solution.py:73
  285.7 4.6 fusion.82
  293.4 28.9 %reduce-scatter.9.cloned.1.call-done = f32[128,1024]{1,0:T(8,128)} async-done(((f32[512,1024]{1,0:T(8,128)}), f32[128,1024]{1,0:T(8,128)}) %reduce-scatter.9.cloned.1.call-update) | async-done | bytes 524304 | tf_op jit(solution)/shard_map/reduce_scatter | solution.py:77
  324.7 4.2 convolution_convert_fusion
  332.2 4.2 convolution_convert_fusion.1
  336.5 4.5 concatenate.32
  341.0 4.6 pad_maximum_fusion
  345.6 9.2 %all-to-all-start.1 = ((bf16[32,8,8192]{2,1,0:T(8,128)(2,1)}), bf16[32,8,8192]{2,1,0:T(8,128)(2,1)}, u32[]{:S(2)}, u32[]{:S(2)}) async-start(bf16[32,8,8192]{2,1,0:T(8,128)(2,1)} %pad_maximum_fusion), calls=%async_computation.5 | async-start | bytes 8388608 | tf_op jit(solution)/shard_map/all_to_all | solution.py:173
  362.0 7.4 %fusion.29 = bf16[4,64,512]{2,1,0:T(8,128)(2,1)S(1)} fusion(bf16[512,4,64]{0,2,1:T(8,128)(2,1)S(1)} %bitcast.116, f32[4,512,512]{1,2,0:T(8,128)} %fusion.84, f32[4,512,512]{1,2,0:T(8,128)} %copy-done.30, f32[4,512]{1,0:T(4,128)S(1)} %log.8, pred[512,512]{0,1:T(8,128)(4,1)S(1)} %copy-done.14), kind=kOutput, calls=%fused_computation.33 | convolution fusion | flops 145885696 | bytes 9183232 | tf_op jit(solution)/shard_map/shqk,sqhe->skhe/dot_general | solution.py:197
  369.5 8.8 %fusion.79 = (bf16[4,64]{1,0:T(4,128)(2,1)S(1)}, bf16[1,512,4,64]{1,3,2,0:T(8,128)(2,1)S(1)}) fusion(bf16[512,4,64]{0,2,1:T(8,128)(2,1)S(1)} %bitcast.114, f32[4,512,512]{1,2,0:T(8,128)} %fusion.84, f32[4,512]{1,0:T(4,128)S(1)} %log.8, f32[4,512,512]{1,2,0:T(8,128)} %copy-done.30, pred[512,512]{0,1:T(8,128)(4,1)S(1)} %copy-done.14), kind=kOutput, calls=%fused_computation.145 | convolution fusion | flops 146016512 | bytes 9183744 | tf_op jit(solution)/shard_map/shqk,skhe->sqhe/dot_general | solution.py:194
  399.4 9.7 %all-to-all-done.1 = bf16[32,8,8192]{2,1,0:T(8,128)(2,1)} async-done(((bf16[32,8,8192]{2,1,0:T(8,128)(2,1)}), bf16[32,8,8192]{2,1,0:T(8,128)(2,1)}, u32[]{:S(2)}, u32[]{:S(2)}) %all-to-all-start.1) | async-done | bytes 4194336 | tf_op jit(solution)/shard_map/all_to_all | solution.py:173
  409.2 7.0 %all-to-all-start = ((bf16[32,8,7296]{2,1,0:T(8,128)(2,1)}), bf16[32,8,7296]{2,1,0:T(8,128)(2,1)}, u32[]{:S(2)}, u32[]{:S(2)}) async-start(bf16[32,8,7296]{2,1,0:T(8,128)(2,1)} %bitcast.97), calls=%async_computation.4 | async-start | bytes 7471104 | tf_op jit(solution)/shard_map/all_to_all | solution.py:232
  421.8 39.6 %all-to-all-done = bf16[32,8,7296]{2,1,0:T(8,128)(2,1)} async-done(((bf16[32,8,7296]{2,1,0:T(8,128)(2,1)}), bf16[32,8,7296]{2,1,0:T(8,128)(2,1)}, u32[]{:S(2)}, u32[]{:S(2)}) %all-to-all-start) | async-done | bytes 3735584 | tf_op jit(solution)/shard_map/all_to_all | solution.py:232
  464.2 17.7 %all-gather.1 = bf16[495616]{0:T(1024)(128)(2,1)} all-gather(bf16[123904]{0:T(1024)(128)(2,1)S(1)} %pad_maximum_fusion.5), channel_id=3, replica_groups=mesh['rep'=4,'shard'=32] {'rep'}, dimensions={0}, use_global_device_ids=true | all-gather | bytes 1239040 | tf_op jit(solution)/shard_map/all_gather | solution.py:235
  494.5 4.5 broadcast_in_dim_reshape.20
  (234 shorter events, 106.7 us)
Async XLA Ops:
  7.2 7.0 %copy-start = (bf16[1,128,1024]{2,1,0:T(8,128)(2,1)S(1)}, bf16[1,128,1024]{2,1,0:T(8,128)(2,1)}, u32[]{:S(2)}) copy-start(bf16[1,128,1024]{2,1,0:T(8,128)(2,1)} %param.16) | copy-start | bytes 786436
  7.2 28.4 %all-gather.8.cloned.1.call-start = ((), (), s32[]{:S(2)}) async-start(), calls=%async_computation.6 | async-start | bytes 1474560 | tf_op jit(solution)/shard_map/all_gather | solution.py:73
  9.9 132.0 %all-gather.16.cloned.1.call-start = ((), (), s32[]{:S(2)}) async-start(), calls=%async_computation.14 | async-start | bytes 8177664 | tf_op jit(solution)/shard_map/all_gather | solution.py:100
  17.1 181.2 %reduce-scatter.5.cloned.1.call-start = ((), (), s32[]{:S(2)}) async-start(), calls=%async_computation.7 | async-start | bytes 2621440 | tf_op jit(solution)/shard_map/reduce_scatter | solution.py:77
  168.5 29.9 %copy-start.8 = (f32[1,128,1024]{2,1,0:T(8,128)S(1)}, f32[1,128,1024]{2,1,0:T(8,128)}, u32[]{:S(2)}) copy-start(f32[1,128,1024]{2,1,0:T(8,128)} %param.10) | copy-start | bytes 1572868
  171.5 51.2 %all-gather.10.cloned.1.call-start = ((), (), s32[]{:S(2)}) async-start(), calls=%async_computation.8 | async-start | bytes 1310720 | tf_op jit(solution)/shard_map/all_gather | solution.py:73
  200.6 59.4 %reduce-scatter.7.cloned.1.call-start = ((), (), s32[]{:S(2)}) async-start(), calls=%async_computation.9 | async-start | bytes 2621440 | tf_op jit(solution)/shard_map/reduce_scatter | solution.py:77
  208.6 19.6 %copy-start.7 = (bf16[1024,1024]{1,0:T(8,128)(2,1)S(1)}, bf16[1024,1024]{1,0:T(8,128)(2,1)}, u32[]{:S(2)}) copy-start(bf16[1024,1024]{1,0:T(8,128)(2,1)} %reshape.371) | copy-start | bytes 6291460
  230.8 30.8 %copy-start.5 = (f32[1,128,1024]{2,1,0:T(8,128)S(1)}, f32[1,128,1024]{2,1,0:T(8,128)}, u32[]{:S(2)}) copy-start(f32[1,128,1024]{2,1,0:T(8,128)} %param.12) | copy-start | bytes 1572868
  230.8 54.9 %all-gather.12.cloned.1.call-start = ((), (), s32[]{:S(2)}) async-start(), calls=%async_computation.10 | async-start | bytes 1310720 | tf_op jit(solution)/shard_map/all_gather | solution.py:73
  263.7 58.6 %reduce-scatter.9.cloned.1.call-start = ((), (), s32[]{:S(2)}) async-start(), calls=%async_computation.11 | async-start | bytes 2621440 | tf_op jit(solution)/shard_map/reduce_scatter | solution.py:77
  293.1 62.5 %all-gather.14.cloned.1.call-start = ((), (), s32[]{:S(2)}) async-start(), calls=%async_computation.12 | async-start | bytes 1310720 | tf_op jit(solution)/shard_map/all_gather | solution.py:73
  345.6 63.6 %all-to-all-start.1 = ((bf16[32,8,8192]{2,1,0:T(8,128)(2,1)}), bf16[32,8,8192]{2,1,0:T(8,128)(2,1)}, u32[]{:S(2)}, u32[]{:S(2)}) async-start(bf16[32,8,8192]{2,1,0:T(8,128)(2,1)} %pad_maximum_fusion), calls=%async_computation.5 | async-start | bytes 8388608 | tf_op jit(solution)/shard_map/all_to_all | solution.py:173
  362.0 16.3 %copy-start.24 = (bf16[1,512,4,64]{1,3,2,0:T(8,128)(2,1)}, bf16[1,512,4,64]{1,3,2,0:T(8,128)(2,1)S(1)}, u32[]{:S(2)}) copy-start(bf16[1,512,4,64]{1,3,2,0:T(8,128)(2,1)S(1)} %get-tuple-element.43) | copy-start | bytes 786436
  362.0 7.5 %copy-start.16 = (bf16[512,256]{0,1:T(8,128)(2,1)S(1)}, bf16[512,256]{0,1:T(8,128)(2,1)}, u32[]{:S(2)}) copy-start(bf16[512,256]{0,1:T(8,128)(2,1)} %copy-done.15) | copy-start | bytes 786436
  369.5 8.9 %copy-start.26 = (bf16[4,64,512]{2,1,0:T(8,128)(2,1)}, bf16[4,64,512]{2,1,0:T(8,128)(2,1)S(1)}, u32[]{:S(2)}) copy-start(bf16[4,64,512]{2,1,0:T(8,128)(2,1)S(1)} %fusion.29) | copy-start | bytes 786436
  369.5 8.9 %copy-start.20 = (bf16[512,1152]{1,0:T(8,128)(2,1)S(1)}, bf16[512,1152]{1,0:T(8,128)(2,1)}, u32[]{:S(2)}) copy-start(bf16[512,1152]{1,0:T(8,128)(2,1)} %all-gather.8.cloned.1.call-done) | copy-start | bytes 3538948
  409.2 7.3 %copy-start.11 = (bf16[1024,768]{1,0:T(8,128)(2,1)S(1)}, bf16[1024,768]{1,0:T(8,128)(2,1)}, u32[]{:S(2)}) copy-start(bf16[1024,768]{1,0:T(8,128)(2,1)} %copy-done.10) | copy-start | bytes 4718596
  409.2 7.3 %copy-start.25 = (bf16[1,512,4,64]{1,3,2,0:T(8,128)(2,1)S(1)}, bf16[1,512,4,64]{1,3,2,0:T(8,128)(2,1)}, u32[]{:S(2)}) copy-start(bf16[1,512,4,64]{1,3,2,0:T(8,128)(2,1)} %copy-done.24) | copy-start | bytes 786436
  409.2 7.3 %copy-start.27 = (bf16[4,64,512]{2,1,0:T(8,128)(2,1)S(1)}, bf16[4,64,512]{2,1,0:T(8,128)(2,1)}, u32[]{:S(2)}) copy-start(bf16[4,64,512]{2,1,0:T(8,128)(2,1)} %copy-done.26) | copy-start | bytes 786436
  409.2 7.3 %copy-start.29 = (bf16[1,512,4,64]{1,3,2,0:T(8,128)(2,1)S(1)}, bf16[1,512,4,64]{1,3,2,0:T(8,128)(2,1)}, u32[]{:S(2)}) copy-start(bf16[1,512,4,64]{1,3,2,0:T(8,128)(2,1)} %copy-done.28) | copy-start | bytes 786436
  409.2 52.2 %all-to-all-start = ((bf16[32,8,7296]{2,1,0:T(8,128)(2,1)}), bf16[32,8,7296]{2,1,0:T(8,128)(2,1)}, u32[]{:S(2)}, u32[]{:S(2)}) async-start(bf16[32,8,7296]{2,1,0:T(8,128)(2,1)} %bitcast.97), calls=%async_computation.4 | async-start | bytes 7471104 | tf_op jit(solution)/shard_map/all_to_all | solution.py:232
  416.2 87.9 %reduce-scatter.11.cloned.1.call-start = ((), (), s32[]{:S(2)}) async-start(), calls=%async_computation.13 | async-start | bytes 2621440 | tf_op jit(solution)/shard_map/reduce_scatter | solution.py:77
  494.5 11.5 %copy-start.1 = (bf16[1,128,1024]{2,1,0:T(8,128)(2,1)S(1)}, bf16[1,128,1024]{2,1,0:T(8,128)(2,1)}, u32[]{:S(2)}) copy-start(bf16[1,128,1024]{2,1,0:T(8,128)(2,1)} %param.16) | copy-start | bytes 786436
  (22 other events, 79.8 us)
Sparse Core Ops, SparseCore 0:
  10.3 25.2 all-gather.7
  39.3 102.5 all-gather.15
  171.6 26.7 reduce-scatter.4
  200.8 21.8 all-gather.9
  231.0 29.0 reduce-scatter.6
  263.8 21.8 all-gather.11
  293.2 29.0 reduce-scatter.8
  324.8 21.8 all-gather.13
  419.5 60.7 reduce-scatter.10
where the time goes:
time: 522 us; the launch traced here: 513 us
  waiting for transfers between devices  292 us (56%)
  local copies, waits for them, and re-layouts  83.9 us (16%)
  matrix products  58.5 us (11%)
  other arithmetic  28.9 us (6%)
  blocking collectives  17.7 us (3%)
  starting transfers between devices  17.3 us (3%)
  between operations  14.8 us (3%)
    all_gather x1, waiting for transfers between devices, local(): gathered = lax.all_gather(packed, 'shard', axis=0, tiled=False)  104 us
    reduce_scatter x4, waiting for transfers between devices, scatter_rep(): return lax.psum_scatter(tensor, 'rep', scatter_dimension=0, tiled=True)  83.3 us
    all_gather x4, waiting for transfers between devices, gather_rep(): return lax.all_gather(tensor, 'rep', axis=0, tiled=True)  54.5 us
    all_to_all x1, waiting for transfers between devices, local(): received = lax.all_to_all(grad_pack, 'shard', 0, 0, tiled=True)  39.6 us
    all_gather x1, blocking collectives, local(): lax.all_gather(all_shares, 'rep', axis=0, tiled=False).astype(jnp.float32)  17.7 us
    dot_general x4, matrix products, matmul(): return jnp.dot(first_op, second_op, preferred_element_type=jnp.float32)  12.3 us
    dot_general x4, matrix products, matmul_lt(): lax.dot_general(first_op, second_op, (((0,), (0,)), ((), ())), preferred_...  12 us
    unnamed x83, local copies, waits for them, and re-layouts  11.9 us
  transfers between devices with their start and end apart: 11, of which 9 were waited for; matrix products, arithmetic and copies ran while one was open for 22% of the time, Pallas kernels for 0%

commit v1 on v0

--- a/solution.py
+++ b/solution.py
@@ -70,7 +70,9 @@
 
 
 def gather_rep(tensor):
-    return lax.all_gather(tensor, "rep", axis=0, tiled=True)
+    return jnp.concatenate(
+        lax.all_to_all(jnp.stack([tensor] * lax.axis_size("rep")), "rep", 0, 0), axis=0
+    )
 
 
 def scatter_rep(tensor):

time: 522 us -> 493 us (0.944)
  waiting for transfers between devices: 292 us -> 225 us
  blocking collectives: 17.7 us -> 35.4 us
  starting transfers between devices: 17.3 us -> 32.7 us
  local copies, waits for them, and re-layouts: 83.9 us -> 94.4 us
    all_gather x4 -> x0, waiting for transfers between devices: 54.5 us -> none  [gather_rep(): return lax.all_gather(tensor, 'rep', axis=0, tiled=True)]
    all_to_all x0 -> x3, waiting for transfers between devices: none -> 31.6 us  [gather_rep(): lax.all_to_all(jnp.stack([tensor] * lax.axis_size('rep')), 'rep', 0, 0)]
    all_gather x1, waiting for transfers between devices: 104 us -> 79.8 us  [local(): gathered = lax.all_gather(packed, 'shard', axis=0, tiled=False)]
    all_to_all x0 -> x1, blocking collectives: none -> 17 us  [gather_rep(): lax.all_to_all(jnp.stack([tensor] * lax.axis_size('rep')), 'rep', 0, 0)]
    reduce_scatter x4, waiting for transfers between devices: 83.3 us -> 67.8 us  [scatter_rep(): return lax.psum_scatter(tensor, 'rep', scatter_dimension=0, tiled=True)]
    all_to_all x0 -> x3, starting transfers between devices: none -> 14.1 us  [gather_rep(): lax.all_to_all(jnp.stack([tensor] * lax.axis_size('rep')), 'rep', 0, 0)]
    unnamed x83 -> x89, local copies, waits for them, and re-layouts: 11.9 us -> 12.7 us
  transfers between devices with their start and end apart: 11 -> 10, of which waited for: 9 -> 9; matrix products, arithmetic and copies ran while one was open for 22% -> 23% of each run, Pallas kernels for 0% -> 0%
where the time goes in v1:
time: 493 us; the launch traced here: 487 us
  waiting for transfers between devices  225 us (46%)
  local copies, waits for them, and re-layouts  94.4 us (19%)
  matrix products  59.5 us (12%)
  blocking collectives  35.4 us (7%)
  starting transfers between devices  32.7 us (7%)
  other arithmetic  26.2 us (5%)
  between operations  14.7 us (3%)
    all_gather x1, waiting for transfers between devices, local(): gathered = lax.all_gather(packed, 'shard', axis=0, tiled=False)  79.8 us
    reduce_scatter x4, waiting for transfers between devices, scatter_rep(): return lax.psum_scatter(tensor, 'rep', scatter_dimension=0, tiled=True)  67.8 us
    all_to_all x1, waiting for transfers between devices, local(): received = lax.all_to_all(grad_pack, 'shard', 0, 0, tiled=True)  39.4 us
    all_to_all x3, waiting for transfers between devices, gather_rep(): lax.all_to_all(jnp.stack([tensor] * lax.axis_size('rep')), 'rep', 0, 0)  31.6 us
    all_gather x1, blocking collectives, local(): lax.all_gather(all_shares, 'rep', axis=0, tiled=False).astype(jnp.float32)  18.4 us
    all_to_all x1, blocking collectives, gather_rep(): lax.all_to_all(jnp.stack([tensor] * lax.axis_size('rep')), 'rep', 0, 0)  17 us
    all_to_all x3, starting transfers between devices, gather_rep(): lax.all_to_all(jnp.stack([tensor] * lax.axis_size('rep')), 'rep', 0, 0)  14.1 us
    dot_general x4, matrix products, matmul(): return jnp.dot(first_op, second_op, preferred_element_type=jnp.float32)  14 us
  transfers between devices with their start and end apart: 10, of which 9 were waited for; matrix products, arithmetic and copies ran while one was open for 23% of the time, Pallas kernels for 0%

profile of v1, /device:TPU:1, one launch (start us, length us, event | category | flops | bytes accessed | tf_op | source)
XLA Modules:
  0.0 487.4 jit_solution(14878913216126134870)
XLA Ops:
  17.8 4.9 %all-to-all-start = ((bf16[4,128,1152]{1,2,0:T(8,128)(2,1)}), bf16[4,128,1152]{1,2,0:T(8,128)(2,1)S(1)}, u32[]{:S(2)}, u32[]{:S(2)}) async-start(bf16[4,128,1152]{1,2,0:T(8,128)(2,1)} %stack.62), calls=%async_computation | async-start | bytes 2359296 | tf_op jit(solution)/shard_map/all_to_all | solution.py:74
  23.0 16.6 %all-to-all-done = bf16[4,128,1152]{1,2,0:T(8,128)(2,1)S(1)} async-done(((bf16[4,128,1152]{1,2,0:T(8,128)(2,1)}), bf16[4,128,1152]{1,2,0:T(8,128)(2,1)S(1)}, u32[]{:S(2)}, u32[]{:S(2)}) %all-to-all-start) | async-done | bytes 1179680 | tf_op jit(solution)/shard_map/all_to_all | solution.py:74
  42.9 79.8 %all-gather.4.cloned.1.call-done = bf16[3964928]{0:T(1024)(128)(2,1)} async-done(((bf16[123904]{0:T(1024)(128)(2,1)}), bf16[3964928]{0:T(1024)(128)(2,1)}) %all-gather.4.cloned.1.call-update) | async-done | bytes 7929872 | tf_op jit(solution)/shard_map/all_gather | solution.py:102
  122.7 8.3 %reshape.418 = bf16[32,123904]{1,0:T(8,128)(2,1)} reshape(bf16[3964928]{0:T(1024)(128)(2,1)} %all-gather.4.cloned.1.call-done) | data formatting | bytes 15859712 | tf_op jit(solution)/shard_map/all_gather | solution.py:102
  131.9 5.8 %fusion.76 = (bf16[32,32768]{1,0:T(8,128)(2,1)}, bf16[32,32768]{1,0:T(8,128)(2,1)}, bf16[32,32768]{1,0:T(8,128)(2,1)}) fusion(bf16[32,123904]{1,0:T(8,128)(2,1)} %reshape.418), kind=kLoop, calls=%fused_computation.142 | loop fusion | bytes 12582912 | tf_op jit(solution)/shard_map/slice | solution.py:103
  160.5 25.4 %reduce-scatter.5.cloned.1.call-done = f32[128,1024]{1,0:T(8,128)} async-done(((f32[512,1024]{1,0:T(8,128)}), f32[128,1024]{1,0:T(8,128)}) %reduce-scatter.5.cloned.1.call-update) | async-done | bytes 524304 | tf_op jit(solution)/shard_map/reduce_scatter | solution.py:79
  188.7 4.6 all-to-all-start.1
  200.7 6.2 %all-to-all-done.1 = bf16[4,128,1024]{2,1,0:T(8,128)(2,1)} async-done(((bf16[4,128,1024]{2,1,0:T(8,128)(2,1)}), bf16[4,128,1024]{2,1,0:T(8,128)(2,1)}, u32[]{:S(2)}, u32[]{:S(2)}) %all-to-all-start.1) | async-done | bytes 1048608 | tf_op jit(solution)/shard_map/all_to_all | solution.py:74
  207.0 4.7 multiply_convert_fusion.1
  214.6 29.6 %reduce-scatter.7.cloned.1.call-done = f32[128,1024]{1,0:T(8,128)} async-done(((f32[512,1024]{1,0:T(8,128)}), f32[128,1024]{1,0:T(8,128)}) %reduce-scatter.7.cloned.1.call-update) | async-done | bytes 524304 | tf_op jit(solution)/shard_map/reduce_scatter | solution.py:79
  247.2 17.0 %all_to_all.30 = bf16[4,128,1024]{2,1,0:T(8,128)(2,1)S(1)} all-to-all(bf16[4,128,1024]{2,1,0:T(8,128)(2,1)S(1)} %stack.64), channel_id=1, replica_groups=mesh['rep'=4,'shard'=32] {'rep'}, dimensions={0} | all-to-all | bytes 2097152 | tf_op jit(solution)/shard_map/all_to_all | solution.py:74
  282.6 4.5 concatenate.32
  287.4 12.7 %reduce-scatter.9.cloned.1.call-done = f32[128,1024]{1,0:T(8,128)} async-done(((f32[512,1024]{1,0:T(8,128)}), f32[128,1024]{1,0:T(8,128)}) %reduce-scatter.9.cloned.1.call-update) | async-done | bytes 524304 | tf_op jit(solution)/shard_map/reduce_scatter | solution.py:79
  302.9 4.6 all-to-all-start.3
  307.5 4.6 pad_maximum_fusion
  312.4 8.8 %all-to-all-done.3 = bf16[4,128,1024]{2,1,0:T(8,128)(2,1)} async-done(((bf16[4,128,1024]{2,1,0:T(8,128)(2,1)}), bf16[4,128,1024]{2,1,0:T(8,128)(2,1)}, u32[]{:S(2)}, u32[]{:S(2)}) %all-to-all-start.3) | async-done | bytes 1048608 | tf_op jit(solution)/shard_map/all_to_all | solution.py:74
  321.2 9.4 %all-to-all-start.5 = ((bf16[32,8,8192]{2,1,0:T(8,128)(2,1)}), bf16[32,8,8192]{2,1,0:T(8,128)(2,1)}, u32[]{:S(2)}, u32[]{:S(2)}) async-start(bf16[32,8,8192]{2,1,0:T(8,128)(2,1)} %pad_maximum_fusion), calls=%async_computation.9 | async-start | bytes 8388608 | tf_op jit(solution)/shard_map/all_to_all | solution.py:175
  337.3 7.4 %fusion.29 = bf16[4,64,512]{2,1,0:T(8,128)(2,1)S(1)} fusion(bf16[512,4,64]{0,2,1:T(8,128)(2,1)S(1)} %bitcast.125, f32[4,512,512]{1,2,0:T(8,128)} %fusion.84, f32[4,512,512]{1,2,0:T(8,128)} %copy-done.32, f32[4,512]{1,0:T(4,128)S(1)} %log.8, pred[512,512]{0,1:T(8,128)(4,1)S(1)} %copy-done.20), kind=kOutput, calls=%fused_computation.33 | convolution fusion | flops 145885696 | bytes 9183232 | tf_op jit(solution)/shard_map/shqk,sqhe->skhe/dot_general | solution.py:199
  344.7 8.8 %fusion.79 = (bf16[4,64]{1,0:T(4,128)(2,1)S(1)}, bf16[1,512,4,64]{1,3,2,0:T(8,128)(2,1)S(1)}) fusion(bf16[512,4,64]{0,2,1:T(8,128)(2,1)S(1)} %bitcast.123, f32[4,512,512]{1,2,0:T(8,128)} %fusion.84, f32[4,512]{1,0:T(4,128)S(1)} %log.8, f32[4,512,512]{1,2,0:T(8,128)} %copy-done.32, pred[512,512]{0,1:T(8,128)(4,1)S(1)} %copy-done.20), kind=kOutput, calls=%fused_computation.145 | convolution fusion | flops 146016512 | bytes 9183744 | tf_op jit(solution)/shard_map/shqk,skhe->sqhe/dot_general | solution.py:196
  375.9 6.0 %all-to-all-done.5 = bf16[32,8,8192]{2,1,0:T(8,128)(2,1)} async-done(((bf16[32,8,8192]{2,1,0:T(8,128)(2,1)}), bf16[32,8,8192]{2,1,0:T(8,128)(2,1)}, u32[]{:S(2)}, u32[]{:S(2)}) %all-to-all-start.5) | async-done | bytes 4194336 | tf_op jit(solution)/shard_map/all_to_all | solution.py:175
  381.8 8.5 %all-to-all-start.4 = ((bf16[32,8,7296]{2,1,0:T(8,128)(2,1)}), bf16[32,8,7296]{2,1,0:T(8,128)(2,1)}, u32[]{:S(2)}, u32[]{:S(2)}) async-start(bf16[32,8,7296]{2,1,0:T(8,128)(2,1)} %bitcast.101), calls=%async_computation.8 | async-start | bytes 7471104 | tf_op jit(solution)/shard_map/all_to_all | solution.py:234
  395.9 39.4 %all-to-all-done.4 = bf16[32,8,7296]{2,1,0:T(8,128)(2,1)} async-done(((bf16[32,8,7296]{2,1,0:T(8,128)(2,1)}), bf16[32,8,7296]{2,1,0:T(8,128)(2,1)}, u32[]{:S(2)}, u32[]{:S(2)}) %all-to-all-start.4) | async-done | bytes 3735584 | tf_op jit(solution)/shard_map/all_to_all | solution.py:234
  438.1 18.4 %all-gather.1 = bf16[495616]{0:T(1024)(128)(2,1)} all-gather(bf16[123904]{0:T(1024)(128)(2,1)S(1)} %pad_maximum_fusion.5), channel_id=3, replica_groups=mesh['rep'=4,'shard'=32] {'rep'}, dimensions={0}, use_global_device_ids=true | all-gather | bytes 1239040 | tf_op jit(solution)/shard_map/all_gather | solution.py:237
  469.2 4.5 broadcast_in_dim_reshape.20
  (241 shorter events, 132.1 us)
Async XLA Ops:
  7.2 7.4 %copy-start.24 = (bf16[1,6,32]{2,1,0:T(8,128)(2,1)S(1)}, bf16[1,6,32]{2,1,0:T(8,128)(2,1)}, u32[]{:S(2)}) copy-start(bf16[1,6,32]{2,1,0:T(8,128)(2,1)} %param.17) | copy-start | bytes 1156
  7.2 7.5 %copy-start.26 = (bf16[1,2,32]{2,1,0:T(2,128)(2,1)S(1)}, bf16[1,2,32]{2,1,0:T(2,128)(2,1)}, u32[]{:S(2)}) copy-start(bf16[1,2,32]{2,1,0:T(2,128)(2,1)} %param.18) | copy-start | bytes 388
  7.2 115.5 %all-gather.4.cloned.1.call-start = ((), (), s32[]{:S(2)}) async-start(), calls=%async_computation.14 | async-start | bytes 8177664 | tf_op jit(solution)/shard_map/all_gather | solution.py:102
  8.7 7.5 %copy-start.27 = (s32[1,128]{1,0:T(1,128)S(1)}, s32[1,128]{1,0:T(1,128)}, u32[]{:S(2)}) copy-start(s32[1,128]{1,0:T(1,128)} %param.11) | copy-start | bytes 1540
  8.7 7.5 %copy-start.9 = (f32[1,128,1024]{2,1,0:T(8,128)S(1)}, f32[1,128,1024]{2,1,0:T(8,128)}, u32[]{:S(2)}) copy-start(f32[1,128,1024]{2,1,0:T(8,128)} %param.10) | copy-start | bytes 1572868
  17.8 21.8 %all-to-all-start = ((bf16[4,128,1152]{1,2,0:T(8,128)(2,1)}), bf16[4,128,1152]{1,2,0:T(8,128)(2,1)S(1)}, u32[]{:S(2)}, u32[]{:S(2)}) async-start(bf16[4,128,1152]{1,2,0:T(8,128)(2,1)} %stack.62), calls=%async_computation | async-start | bytes 2359296 | tf_op jit(solution)/shard_map/all_to_all | solution.py:74
  22.7 163.3 %reduce-scatter.5.cloned.1.call-start = ((), (), s32[]{:S(2)}) async-start(), calls=%async_computation.10 | async-start | bytes 2621440 | tf_op jit(solution)/shard_map/reduce_scatter | solution.py:79
  188.7 18.3 %all-to-all-start.1 = ((bf16[4,128,1024]{2,1,0:T(8,128)(2,1)}), bf16[4,128,1024]{2,1,0:T(8,128)(2,1)}, u32[]{:S(2)}, u32[]{:S(2)}) async-start(bf16[4,128,1024]{2,1,0:T(8,128)(2,1)} %stack.63), calls=%async_computation.2 | async-start | bytes 2097152 | tf_op jit(solution)/shard_map/all_to_all | solution.py:74
  193.3 50.9 %reduce-scatter.7.cloned.1.call-start = ((), (), s32[]{:S(2)}) async-start(), calls=%async_computation.11 | async-start | bytes 2621440 | tf_op jit(solution)/shard_map/reduce_scatter | solution.py:79
  214.3 31.4 %copy-start.5 = (f32[1,128,1024]{2,1,0:T(8,128)S(1)}, f32[1,128,1024]{2,1,0:T(8,128)}, u32[]{:S(2)}) copy-start(f32[1,128,1024]{2,1,0:T(8,128)} %param.12) | copy-start | bytes 1572868
  214.3 85.8 %reduce-scatter.9.cloned.1.call-start = ((), (), s32[]{:S(2)}) async-start(), calls=%async_computation.12 | async-start | bytes 2621440 | tf_op jit(solution)/shard_map/reduce_scatter | solution.py:79
  247.1 17.2 %copy-start.8 = (bf16[1024,1024]{1,0:T(8,128)(2,1)S(1)}, bf16[1024,1024]{1,0:T(8,128)(2,1)}, u32[]{:S(2)}) copy-start(bf16[1024,1024]{1,0:T(8,128)(2,1)} %reshape.393) | copy-start | bytes 6291460
  247.1 17.2 %copy-start.35 = (f32[512,1024]{1,0:T(8,128)S(1)}, f32[512,1024]{1,0:T(8,128)}, u32[]{:S(2)}) copy-start(f32[512,1024]{1,0:T(8,128)} %get-tuple-element.49) | copy-start | bytes 6291460
  302.9 18.3 %all-to-all-start.3 = ((bf16[4,128,1024]{2,1,0:T(8,128)(2,1)}), bf16[4,128,1024]{2,1,0:T(8,128)(2,1)}, u32[]{:S(2)}, u32[]{:S(2)}) async-start(bf16[4,128,1024]{2,1,0:T(8,128)(2,1)} %stack.65), calls=%async_computation.6 | async-start | bytes 2097152 | tf_op jit(solution)/shard_map/all_to_all | solution.py:74
  321.2 60.6 %all-to-all-start.5 = ((bf16[32,8,8192]{2,1,0:T(8,128)(2,1)}), bf16[32,8,8192]{2,1,0:T(8,128)(2,1)}, u32[]{:S(2)}, u32[]{:S(2)}) async-start(bf16[32,8,8192]{2,1,0:T(8,128)(2,1)} %pad_maximum_fusion), calls=%async_computation.9 | async-start | bytes 8388608 | tf_op jit(solution)/shard_map/all_to_all | solution.py:175
  337.3 7.4 %copy-start.22 = (bf16[512,256]{0,1:T(8,128)(2,1)S(1)}, bf16[512,256]{0,1:T(8,128)(2,1)}, u32[]{:S(2)}) copy-start(bf16[512,256]{0,1:T(8,128)(2,1)} %copy-done.21) | copy-start | bytes 786436
  344.7 8.9 %copy-start.28 = (bf16[4,64,512]{2,1,0:T(8,128)(2,1)}, bf16[4,64,512]{2,1,0:T(8,128)(2,1)S(1)}, u32[]{:S(2)}) copy-start(bf16[4,64,512]{2,1,0:T(8,128)(2,1)S(1)} %fusion.29) | copy-start | bytes 786436
  344.7 8.9 %copy-start.12 = (bf16[4,128,1152]{2,1,0:T(8,128)(2,1)S(1)}, bf16[4,128,1152]{2,1,0:T(8,128)(2,1)}, u32[]{:S(2)}) copy-start(bf16[4,128,1152]{2,1,0:T(8,128)(2,1)} %copy.72) | copy-start | bytes 3538948
  381.8 8.8 %copy-start.11 = (bf16[1024,768]{1,0:T(8,128)(2,1)S(1)}, bf16[1024,768]{1,0:T(8,128)(2,1)}, u32[]{:S(2)}) copy-start(bf16[1024,768]{1,0:T(8,128)(2,1)} %reshape.383) | copy-start | bytes 4718596
  381.8 8.8 %copy-start.29 = (bf16[4,64,512]{2,1,0:T(8,128)(2,1)S(1)}, bf16[4,64,512]{2,1,0:T(8,128)(2,1)}, u32[]{:S(2)}) copy-start(bf16[4,64,512]{2,1,0:T(8,128)(2,1)} %copy-done.28) | copy-start | bytes 786436
  381.8 8.8 %copy-start.31 = (bf16[1,512,4,64]{1,3,2,0:T(8,128)(2,1)S(1)}, bf16[1,512,4,64]{1,3,2,0:T(8,128)(2,1)}, u32[]{:S(2)}) copy-start(bf16[1,512,4,64]{1,3,2,0:T(8,128)(2,1)} %copy-done.30) | copy-start | bytes 786436
  381.8 53.5 %all-to-all-start.4 = ((bf16[32,8,7296]{2,1,0:T(8,128)(2,1)}), bf16[32,8,7296]{2,1,0:T(8,128)(2,1)}, u32[]{:S(2)}, u32[]{:S(2)}) async-start(bf16[32,8,7296]{2,1,0:T(8,128)(2,1)} %bitcast.101), calls=%async_computation.8 | async-start | bytes 7471104 | tf_op jit(solution)/shard_map/all_to_all | solution.py:234
  390.3 88.4 %reduce-scatter.11.cloned.1.call-start = ((), (), s32[]{:S(2)}) async-start(), calls=%async_computation.13 | async-start | bytes 2621440 | tf_op jit(solution)/shard_map/reduce_scatter | solution.py:79
  469.2 11.5 %copy-start.1 = (bf16[1,128,1024]{2,1,0:T(8,128)(2,1)S(1)}, bf16[1,128,1024]{2,1,0:T(8,128)(2,1)}, u32[]{:S(2)}) copy-start(bf16[1,128,1024]{2,1,0:T(8,128)(2,1)} %param.16) | copy-start | bytes 786436
  (24 other events, 81.9 us)
Sparse Core Ops, SparseCore 0:
  16.3 106.3 all-gather.3
  159.3 26.6 reduce-scatter.4
  214.5 29.6 reduce-scatter.6
  270.3 29.8 reduce-scatter.8
  393.4 61.6 reduce-scatter.10
